TPU v7x, 32 devices: a whole 2x2x4 slice. The times are simulated.
32 devices in a mesh: dp: 8 (over y, x, core), seq: 4 (over z).
Axes of the slice: x: 2, y: 2, z: 4, core: 2. Of those that a mesh axis runs over, the one named last changes fastest.
Arguments:
- inputs: bfloat16 [8, 1024, 768], P('dp', 'seq'), may hold values from -6 to 6
- block_ids: int32 [8, 4], P('dp'), may hold values from 0 to 1, never falling along the last dimension, each value on 1 to 3 neighbouring positions
- query_weight: bfloat16 [768, 768], P('dp'), may hold values from -0.3125 to 0.3125
- query_bias: bfloat16 [768], P('dp'), may hold values from -3 to 3
- key_weight: bfloat16 [768, 768], P('dp'), may hold values from -0.3125 to 0.3125
- value_weight: bfloat16 [768, 768], P('dp'), may hold values from -0.21875 to 0.21875
- value_bias: bfloat16 [768], P('dp'), may hold values from -3 to 3
- output_weight: bfloat16 [768, 768], P('dp'), may hold values from -1.25 to 1.25
- output_bias: bfloat16 [768], P('dp'), may hold values from -3 to 3
- attention_gain: bfloat16 [768], P('dp'), may hold values from 0.5 to 1.5
- attention_shift: bfloat16 [768], P('dp'), may hold values from -2 to 2
- expand_weight: bfloat16 [768, 3072], P('dp'), may hold values from -0.21875 to 0.21875
- expand_bias: bfloat16 [3072], P('dp'), may hold values from -3 to 3
- reduce_weight: bfloat16 [3072, 768], P('dp'), may hold values from -0.109375 to 0.109375
- reduce_bias: bfloat16 [768], P('dp'), may hold values from -3 to 3
- final_gain: bfloat16 [768], P('dp'), may hold values from 0.5 to 1.5
- final_shift: bfloat16 [768], P('dp'), may hold values from -2 to 2
- cotangent: bfloat16 [8, 1024, 768], P('dp', 'seq'), may hold values from -6 to 6
Outputs:
- output: bfloat16 [8, 1024, 768], P('dp', 'seq')
- input_gradient: float32 [8, 1024, 768], P('dp', 'seq')
- query_matrix: float32 [768, 768], P('dp')
- query_vector: float32 [768], P('dp')
- key_matrix: float32 [768, 768], P('dp')
- value_matrix: float32 [768, 768], P('dp')
- value_vector: float32 [768], P('dp')
- output_matrix: float32 [768, 768], P('dp')
- output_vector: float32 [768], P('dp')
- first_scale: float32 [768], P('dp')
- first_offset: float32 [768], P('dp')
- expand_matrix: float32 [768, 3072], P('dp')
- expand_vector: float32 [3072], P('dp')
- reduce_matrix: float32 [3072, 768], P('dp')
- reduce_vector: float32 [768], P('dp')
- last_scale: float32 [768], P('dp')
- last_offset: float32 [768], P('dp')
Inputs may be any that keep to these rules, and one draw needn't show every extreme that they name: block_ids[s, b] is the document of the b-th block of sequence s; two documents in every sequence, each covering 1 to 3 neighbouring blocks (4 in all); numbers never fall along a sequence.
All inputs are finite; a program needn't handle non-finite values.
Results may differ from a plain program's by a relative error of at most 0.018.
Values may be sent and summed in bfloat16 or wider, within the bound.
A program may use at most 128 MiB of HBM per device.

v0:
```python
import functools

import jax
import jax.numpy as jnp
from jax import lax
from jax.experimental import pallas as pl
from jax.experimental.pallas import tpu as pltpu
from jax.sharding import PartitionSpec as P

HD = 64
BLK = 256


EPSILON = 1e-12
MASKED = -1e30
ROW_BLOCK = 512


def as_sent(value):
    return jax.tree.map(lambda a: a.astype(jnp.bfloat16) if a.dtype == jnp.float32 else a, value)


def layer_norm(values, norm_gain, norm_shift):
    middle = jnp.mean(values, axis=-1, keepdims=True)
    centred = values - middle
    spread = jnp.mean(centred * centred, axis=-1, keepdims=True)
    return centred * lax.rsqrt(spread + EPSILON) * norm_gain + norm_shift


def gelu_exact(values):
    return jax.nn.gelu(values, approximate=False)


def product(former, latter):
    return jnp.dot(former, latter, preferred_element_type=jnp.float32)


def left_transposed(former, latter):
    return lax.dot_general(
        former, latter, (((0,), (0,)), ((), ())), preferred_element_type=jnp.float32
    )


def right_transposed(former, latter):
    return lax.dot_general(
        former, latter, (((1,), (1,)), ((), ())), preferred_element_type=jnp.float32
    )


def column_sum(values):
    return jnp.sum(values.astype(jnp.float32), axis=0)


def block_mask(allowed, row_start, row_count, key_reach):
    table_part = allowed[row_start // BLK : (row_start + row_count) // BLK, : key_reach // BLK]
    return jnp.repeat(jnp.repeat(table_part, BLK, axis=0), BLK, axis=1)


def masked_scores(queries, key_rows, allowed, row_start, row_count):
    key_reach = row_start + row_count
    scores = right_transposed(queries[row_start:key_reach], key_rows[:key_reach]) * HD ** (-0.5)
    return jnp.where(block_mask(allowed, row_start, row_count, key_reach), scores, MASKED)


def head_forward(head_item, allowed):
    queries, key_rows, value_rows = head_item
    length = queries.shape[0]
    row_count = min(ROW_BLOCK, length)
    contexts = []
    totals = []
    for row_start in range(0, length, row_count):
        scores = masked_scores(queries, key_rows, allowed, row_start, row_count)
        row_peak = jnp.max(scores, axis=-1, keepdims=True)
        exponent = jnp.exp(scores - row_peak)
        row_total = jnp.sum(exponent, axis=-1, keepdims=True)
        probabilities = (exponent / row_total).astype(jnp.bfloat16)
        contexts.append(
            product(probabilities, value_rows[: row_start + row_count]).astype(jnp.bfloat16)
        )
        totals.append(row_peak[:, 0] + jnp.log(row_total[:, 0]))
    return (jnp.concatenate(contexts, axis=0), jnp.concatenate(totals, axis=0))


def head_backward(head_item, allowed):
    queries, key_rows, value_rows, context_rows, totals = head_item
    length = queries.shape[0]
    row_count = min(ROW_BLOCK, length)
    score_scale = HD ** (-0.5)
    query_parts = []
    key_total = jnp.zeros(key_rows.shape, jnp.float32)
    value_total = jnp.zeros(value_rows.shape, jnp.float32)
    for row_start in range(0, length, row_count):
        key_reach = row_start + row_count
        scores = masked_scores(queries, key_rows, allowed, row_start, row_count)
        probabilities = jnp.exp(scores - totals[row_start:key_reach, None])
        incoming = context_rows[row_start:key_reach]
        back_weights = right_transposed(incoming, value_rows[:key_reach])
        inner_sum = jnp.sum(probabilities * back_weights, axis=-1, keepdims=True)
        back_scores = (probabilities * (back_weights - inner_sum)).astype(jnp.bfloat16)
        query_parts.append(product(back_scores, key_rows[:key_reach]) * score_scale)
        key_total = key_total.at[:key_reach].add(
            left_transposed(back_scores, queries[row_start:key_reach]) * score_scale
        )
        value_total = value_total.at[:key_reach].add(
            left_transposed(probabilities.astype(jnp.bfloat16), incoming)
        )
    back_queries = jnp.concatenate(query_parts, axis=0).astype(jnp.bfloat16)
    return (back_queries, key_total.astype(jnp.bfloat16), value_total.astype(jnp.bfloat16))


def general_shards(
    inputs,
    block_ids,
    query_weight,
    query_bias,
    key_weight,
    value_weight,
    value_bias,
    output_weight,
    output_bias,
    attention_gain,
    attention_shift,
    expand_weight,
    expand_bias,
    reduce_weight,
    reduce_bias,
    final_gain,
    final_shift,
    cotangent,
):
    tokens = inputs[0]
    documents = block_ids[0]
    block_order = jnp.arange(documents.shape[0], dtype=jnp.int32)
    allowed = (documents[:, None] == documents[None, :]) & (
        block_order[None, :] <= block_order[:, None]
    )
    (
        query_full,
        query_shift,
        key_full,
        value_full,
        value_shift,
        output_full,
        output_shift,
        norm_gain,
        norm_shift,
        expand_full,
        expand_shift,
        reduce_full,
        reduce_shift,
        last_gain,
        last_shift,
    ) = (
        lax.all_gather(query_weight, "dp", axis=0, tiled=True),
        lax.all_gather(query_bias, "dp", axis=0, tiled=True),
        lax.all_gather(key_weight, "dp", axis=0, tiled=True),
        lax.all_gather(value_weight, "dp", axis=0, tiled=True),
        lax.all_gather(value_bias, "dp", axis=0, tiled=True),
        lax.all_gather(output_weight, "dp", axis=0, tiled=True),
        lax.all_gather(output_bias, "dp", axis=0, tiled=True),
        lax.all_gather(attention_gain, "dp", axis=0, tiled=True),
        lax.all_gather(attention_shift, "dp", axis=0, tiled=True),
        lax.all_gather(expand_weight, "dp", axis=0, tiled=True),
        lax.all_gather(expand_bias, "dp", axis=0, tiled=True),
        lax.all_gather(reduce_weight, "dp", axis=0, tiled=True),
        lax.all_gather(reduce_bias, "dp", axis=0, tiled=True),
        lax.all_gather(final_gain, "dp", axis=0, tiled=True),
        lax.all_gather(final_shift, "dp", axis=0, tiled=True),
    )
    queries_token = (product(tokens, query_full) + query_shift.astype(jnp.float32)).astype(
        jnp.bfloat16
    )
    keys_token = product(tokens, key_full).astype(jnp.bfloat16)
    values_token = (product(tokens, value_full) + value_shift.astype(jnp.float32)).astype(
        jnp.bfloat16
    )
    stacked = jnp.stack([queries_token, keys_token, values_token])
    spread_heads = lax.all_to_all(stacked, "seq", split_axis=2, concat_axis=1, tiled=True)
    length = spread_heads.shape[1]
    head_count = spread_heads.shape[2] // HD
    by_head = spread_heads.reshape(3, length, head_count, HD).transpose(0, 2, 1, 3)
    contexts, totals = lax.map(
        lambda head_item: head_forward(head_item, allowed), (by_head[0], by_head[1], by_head[2])
    )
    context_rows = contexts.transpose(1, 0, 2).reshape(length, head_count * HD)
    context_token = lax.all_to_all(
        as_sent(context_rows), "seq", split_axis=0, concat_axis=1, tiled=True
    ).astype(context_rows.dtype)
    attended = product(context_token, output_full) + output_shift.astype(jnp.float32)
    first_pre = tokens.astype(jnp.float32) + attended
    hidden, first_pull = jax.vjp(
        layer_norm, first_pre, norm_gain.astype(jnp.float32), norm_shift.astype(jnp.float32)
    )
    hidden_low = hidden.astype(jnp.bfloat16)
    expanded = product(hidden_low, expand_full) + expand_shift.astype(jnp.float32)
    activated, gelu_pull = jax.vjp(gelu_exact, expanded)
    activated_low = activated.astype(jnp.bfloat16)
    reduced = product(activated_low, reduce_full) + reduce_shift.astype(jnp.float32)
    final_pre = hidden_low.astype(jnp.float32) + reduced
    final_out, final_pull = jax.vjp(
        layer_norm, final_pre, last_gain.astype(jnp.float32), last_shift.astype(jnp.float32)
    )
    output = final_out.astype(jnp.bfloat16)[None]
    query_full, key_full, value_full, output_full, expand_full, reduce_full = (
        lax.all_gather(query_weight, "dp", axis=0, tiled=True),
        lax.all_gather(key_weight, "dp", axis=0, tiled=True),
        lax.all_gather(value_weight, "dp", axis=0, tiled=True),
        lax.all_gather(output_weight, "dp", axis=0, tiled=True),
        lax.all_gather(expand_weight, "dp", axis=0, tiled=True),
        lax.all_gather(reduce_weight, "dp", axis=0, tiled=True),
    )
    back_final, last_scale, last_offset = final_pull(cotangent[0].astype(jnp.float32))
    back_reduced = back_final.astype(jnp.bfloat16)
    reduce_matrix = left_transposed(activated_low, back_reduced)
    reduce_vector = column_sum(back_reduced)
    back_activated = right_transposed(back_reduced, reduce_full)
    back_expanded = gelu_pull(back_activated)[0].astype(jnp.bfloat16)
    expand_matrix = left_transposed(hidden_low, back_expanded)
    expand_vector = column_sum(back_expanded)
    back_hidden = back_final + right_transposed(back_expanded, expand_full)
    back_attended, first_scale, first_offset = first_pull(back_hidden)
    attended_low = back_attended.astype(jnp.bfloat16)
    output_matrix = left_transposed(context_token, attended_low)
    output_vector = column_sum(attended_low)
    back_context = right_transposed(attended_low, output_full).astype(jnp.bfloat16)
    context_spread = lax.all_to_all(back_context, "seq", split_axis=1, concat_axis=0, tiled=True)
    context_by_head = context_spread.reshape(length, head_count, HD).transpose(1, 0, 2)
    back_heads = lax.map(
        lambda head_item: head_backward(head_item, allowed),
        (by_head[0], by_head[1], by_head[2], context_by_head, totals),
    )
    back_stacked = jnp.stack(back_heads).transpose(0, 2, 1, 3).reshape(3, length, head_count * HD)
    back_token = lax.all_to_all(
        as_sent(back_stacked), "seq", split_axis=1, concat_axis=2, tiled=True
    ).astype(back_stacked.dtype)
    back_query = back_token[0]
    back_key = back_token[1]
    back_value = back_token[2]
    input_gradient = (
        back_attended
        + right_transposed(back_query, query_full)
        + right_transposed(back_key, key_full)
        + right_transposed(back_value, value_full)
    )
    query_matrix = left_transposed(tokens, back_query)
    query_vector = column_sum(back_query)
    key_matrix = left_transposed(tokens, back_key)
    value_matrix = left_transposed(tokens, back_value)
    value_vector = column_sum(back_value)
    (
        query_matrix,
        query_vector,
        key_matrix,
        value_matrix,
        value_vector,
        output_matrix,
        output_vector,
        first_scale,
        first_offset,
        expand_matrix,
        expand_vector,
        reduce_matrix,
        reduce_vector,
        last_scale,
        last_offset,
    ) = (
        lax.psum_scatter(query_matrix, "dp", scatter_dimension=0, tiled=True),
        lax.psum_scatter(query_vector, "dp", scatter_dimension=0, tiled=True),
        lax.psum_scatter(key_matrix, "dp", scatter_dimension=0, tiled=True),
        lax.psum_scatter(value_matrix, "dp", scatter_dimension=0, tiled=True),
        lax.psum_scatter(value_vector, "dp", scatter_dimension=0, tiled=True),
        lax.psum_scatter(output_matrix, "dp", scatter_dimension=0, tiled=True),
        lax.psum_scatter(output_vector, "dp", scatter_dimension=0, tiled=True),
        lax.psum_scatter(first_scale, "dp", scatter_dimension=0, tiled=True),
        lax.psum_scatter(first_offset, "dp", scatter_dimension=0, tiled=True),
        lax.psum_scatter(expand_matrix, "dp", scatter_dimension=0, tiled=True),
        lax.psum_scatter(expand_vector, "dp", scatter_dimension=0, tiled=True),
        lax.psum_scatter(reduce_matrix, "dp", scatter_dimension=0, tiled=True),
        lax.psum_scatter(reduce_vector, "dp", scatter_dimension=0, tiled=True),
        lax.psum_scatter(last_scale, "dp", scatter_dimension=0, tiled=True),
        lax.psum_scatter(last_offset, "dp", scatter_dimension=0, tiled=True),
    )
    owned = (
        lax.psum(query_matrix.astype(jnp.bfloat16), "seq").astype(jnp.float32),
        lax.psum(query_vector.astype(jnp.bfloat16), "seq").astype(jnp.float32),
        lax.psum(key_matrix.astype(jnp.bfloat16), "seq").astype(jnp.float32),
        lax.psum(value_matrix.astype(jnp.bfloat16), "seq").astype(jnp.float32),
        lax.psum(value_vector.astype(jnp.bfloat16), "seq").astype(jnp.float32),
        lax.psum(output_matrix.astype(jnp.bfloat16), "seq").astype(jnp.float32),
        lax.psum(output_vector.astype(jnp.bfloat16), "seq").astype(jnp.float32),
        lax.psum(first_scale.astype(jnp.bfloat16), "seq").astype(jnp.float32),
        lax.psum(first_offset.astype(jnp.bfloat16), "seq").astype(jnp.float32),
        lax.psum(expand_matrix.astype(jnp.bfloat16), "seq").astype(jnp.float32),
        lax.psum(expand_vector.astype(jnp.bfloat16), "seq").astype(jnp.float32),
        lax.psum(reduce_matrix.astype(jnp.bfloat16), "seq").astype(jnp.float32),
        lax.psum(reduce_vector.astype(jnp.bfloat16), "seq").astype(jnp.float32),
        lax.psum(last_scale.astype(jnp.bfloat16), "seq").astype(jnp.float32),
        lax.psum(last_offset.astype(jnp.bfloat16), "seq").astype(jnp.float32),
    )
    return (output, input_gradient[None]) + tuple(owned)


MESH = pl.DeviceIdType.MESH
KEY, VALUE, QUERY, OUT, EXPAND, REDUCE = range(6)
ROWS = (96, 96, 96, 96, 96, 384)
COLS = (768, 768, 768, 768, 3072, 768)
GATHER_UNITS = (
    [(w, 0, 768, False) for w in (KEY, VALUE, QUERY, OUT)]
    + [(EXPAND, 768 * j, 768, True) for j in range(4)]
    + [(REDUCE, 256 * j, 256, True) for j in range(3)]
)
SUM_UNITS = (
    [(REDUCE, 256 * j, 256) for j in range(3)]
    + [(EXPAND, 768 * j, 768) for j in range(4)]
    + [(w, 0, 768) for w in (OUT, QUERY, KEY, VALUE)]
)
TOKENS = 256
WIDTH = 768


class Place:
    def __init__(self):
        self.d = lax.axis_index("dp")
        self.z = lax.axis_index("seq")
        self.y = self.d // 4
        self.x = (self.d // 2) % 2
        self.c = self.d % 2
        self.parity = self.z % 2
        self.partner_z = self.z + 1 - 2 * self.parity

    def shard(self, flip_y, flip_x, flip_c):
        y = 1 - self.y if flip_y else self.y
        x = 1 - self.x if flip_x else self.x
        c = 1 - self.c if flip_c else self.c
        return 4 * y + 2 * x + c

    def quarter(self, flip_y, flip_x):
        y = 1 - self.y if flip_y else self.y
        x = 1 - self.x if flip_x else self.x
        return 2 * y + x

    def peer(self, kind):
        if kind == "x":
            return (self.shard(0, 1, 0), self.z)
        if kind == "y":
            return (self.shard(1, 0, 0), self.z)
        if kind == "s":
            return (self.shard(0, 0, 1), self.z)
        return (self.d, self.partner_z)


def remote(source, target, send_sem, recv_sem, peer):
    return pltpu.make_async_remote_copy(
        src_ref=source,
        dst_ref=target,
        send_sem=send_sem,
        recv_sem=recv_sem,
        device_id=peer,
        device_id_type=MESH,
    )


class Gather:
    def __init__(self, place, own, full, send_sems, recv_sems):
        self.place, self.own, self.full = place, own, full
        self.send_sems, self.recv_sems = send_sems, recv_sems

    def rows(self, unit, part):
        w, _, _, paired = GATHER_UNITS[unit]
        count = ROWS[w]
        parity = self.place.parity
        if part == "all":
            return pl.ds(0, count)
        if not paired:
            half = count // 2
            return {"a": pl.ds(0, half), "b": pl.ds(half, half), "ab": pl.ds(0, count)}[part]
        third = count // 3
        if part == "a":
            return pl.ds(pl.multiple_of(2 * third * parity, third), third)
        if part == "b":
            return pl.ds(third, third)
        if part == "w":
            return pl.ds(pl.multiple_of(2 * third * (1 - parity), third), third)
        return pl.ds(pl.multiple_of(third * parity, third), 2 * third)

    def slot(self, unit, shard, part):
        w, col, width, _ = GATHER_UNITS[unit]
        return self.full[w].at[shard, self.rows(unit, part), pl.ds(col, width)]

    def copy(self, unit, lane, kind, shard, part, source=None):
        target = self.slot(unit, shard, part)
        return remote(
            target if source is None else source,
            target,
            self.send_sems.at[unit, lane],
            self.recv_sems.at[unit, lane],
            self.place.peer(kind),
        )

    def own_source(self, unit, part):
        w, col, width, _ = GATHER_UNITS[unit]
        return self.own[w].at[self.rows(unit, part), pl.ds(col, width)]

    def sends(self, unit):
        p = self.place
        mine, over_x, over_y, over_d = p.d, p.shard(0, 1, 0), p.shard(1, 0, 0), p.shard(1, 1, 0)
        table = {
            0: ("x", mine, "ab", True),
            1: ("x", over_y, "a", False),
            2: ("y", mine, "ab", True),
            3: ("y", over_x, "b", False),
            4: ("s", mine, "all", True),
            5: ("s", over_x, "ab", False),
            6: ("s", over_y, "ab", False),
            7: ("s", over_d, "ab", False),
        }
        if GATHER_UNITS[unit][3]:
            table.update(
                {
                    8: ("z", over_x, "a", False),
                    9: ("z", over_y, "a", False),
                    10: ("z", over_d, "a", False),
                    11: ("s", over_x, "w", False),
                    12: ("s", over_y, "w", False),
                    13: ("s", over_d, "w", False),
                }
            )
        return table

    def arrivals(self, unit):
        p = self.place
        over_x, over_y, over_d = p.shard(0, 1, 0), p.shard(1, 0, 0), p.shard(1, 1, 0)
        sib, sib_x, sib_y, sib_d = p.shard(0, 0, 1), p.shard(0, 1, 1), p.shard(1, 0, 1), p.shard(1, 1, 1)
        return {
            0: ("x", over_x, "ab"),
            1: ("x", over_d, "a"),
            2: ("y", over_y, "ab"),
            3: ("y", over_d, "b"),
            4: ("s", sib, "all"),
            5: ("s", sib_x, "ab"),
            6: ("s", sib_y, "ab"),
            7: ("s", sib_d, "ab"),
            8: ("z", over_x, "w"),
            9: ("z", over_y, "w"),
            10: ("z", over_d, "w"),
            11: ("s", sib_x, "w"),
            12: ("s", sib_y, "w"),
            13: ("s", sib_d, "w"),
        }

    def start(self, unit, *lanes):
        table = self.sends(unit)
        for lane in lanes:
            if lane in table:
                kind, shard, part, from_own = table[lane]
                source = self.own_source(unit, part) if from_own else None
                self.copy(unit, lane, kind, shard, part, source).start()

    def wait(self, unit, *lanes):
        table = self.sends(unit)
        for lane in lanes:
            if lane in table:
                kind, shard, part = self.arrivals(unit)[lane]
                self.copy(unit, lane, kind, shard, part).wait_recv()

    def open(self, unit):
        if unit < len(GATHER_UNITS):
            self.start(unit, 0, 2, 4)

    def relay(self, unit):
        if 0 <= unit < len(GATHER_UNITS):
            self.wait(unit, 0)
            self.start(unit, 3, 8, 5)
            self.wait(unit, 2)
            self.start(unit, 1, 9, 6)

    def relay_far(self, unit):
        if 0 <= unit < len(GATHER_UNITS):
            self.wait(unit, 1)
            self.start(unit, 10)
            self.wait(unit, 3)
            self.start(unit, 7)
            self.wait(unit, 8)
            self.start(unit, 11)
            self.wait(unit, 9)
            self.start(unit, 12)

    def relay_last(self, unit):
        if 0 <= unit < len(GATHER_UNITS):
            self.wait(unit, 10)
            self.start(unit, 13)

    def arrived(self, unit):
        if 0 <= unit < len(GATHER_UNITS):
            self.wait(unit, 4, 5, 6, 7, 11, 12, 13)

    def drain(self):
        for unit in range(len(GATHER_UNITS)):
            for lane, (kind, shard, part, from_own) in self.sends(unit).items():
                source = self.own_source(unit, part) if from_own else None
                self.copy(unit, lane, kind, shard, part, source).wait_send()


PLANE = [(fy, fx, fc) for fy in (0, 1) for fx in (0, 1) for fc in (0, 1)][1:]


def greet(place):
    barrier = pltpu.get_barrier_semaphore()
    for flips in PLANE:
        pl.semaphore_signal(
            barrier, inc=1, device_id=(place.shard(*flips), place.z), device_id_type=MESH
        )

    @pl.when(place.z > 0)
    def _():
        pl.semaphore_signal(barrier, inc=1, device_id=(place.d, place.z - 1), device_id_type=MESH)

    @pl.when(place.z < 3)
    def _():
        pl.semaphore_signal(barrier, inc=1, device_id=(place.d, place.z + 1), device_id_type=MESH)

    pl.semaphore_wait(barrier, 8 + (place.z * (3 - place.z)) // 2)


def cut(unit, part):
    count = ROWS[SUM_UNITS[unit][0]]
    half = count // 2
    return {"a": pl.ds(0, half), "b": pl.ds(half, half), "all": pl.ds(0, count)}[part]


class Reduce:
    def __init__(self, place, buffers, send_sems, recv_sems):
        self.place = place
        self.chip, self.far, self.near, self.outer, self.inner, self.total = buffers
        self.send_sems, self.recv_sems = send_sems, recv_sems
        self.rim_z = jnp.where(place.z < 2, 0, 3)
        self.core_z = jnp.where(place.z < 2, 1, 2)
        self.is_rim = (place.z == 0) | (place.z == 3)

    def view(self, family, unit, part, *lead):
        w, col, width = SUM_UNITS[unit]
        return family[w].at[(*lead, cut(unit, part), pl.ds(col, width))]

    def copy(self, unit, lane, source, target, peer):
        return remote(
            source, target, self.send_sems.at[unit, lane], self.recv_sems.at[unit, lane], peer
        )

    def sibling(self, unit, source):
        w, col, width = SUM_UNITS[unit]
        return self.copy(
            unit, 0, source, self.chip[w].at[:, :, pl.ds(col, width)], self.place.peer("s")
        )

    def lanes(self, unit):
        p = self.place
        to_x, to_y, to_d = p.quarter(0, 1), p.quarter(1, 0), p.quarter(1, 1)
        c, f, n = self.chip, self.far, self.near
        x, y = p.peer("x"), p.peer("y")
        return {
            1: (self.view(c, unit, "a", to_d), self.view(f, unit, "a"), x),
            2: (self.view(c, unit, "b", to_d), self.view(f, unit, "b"), y),
            3: (self.view(c, unit, "a", to_x), self.view(n, unit, "a", 0), x),
            4: (self.view(c, unit, "b", to_x), self.view(n, unit, "b", 0), x),
            5: (self.view(c, unit, "b", to_y), self.view(n, unit, "b", 1), y),
            6: (self.view(c, unit, "a", to_y), self.view(n, unit, "a", 1), y),
            7: (
                self.view(c, unit, "all", p.quarter(0, 0)),
                self.view(self.outer, unit, "all"),
                (p.d, self.core_z),
            ),
            8: (
                self.view(self.outer, unit, "all"),
                self.view(self.inner, unit, "all"),
                (p.d, 3 - self.core_z),
            ),
            9: (
                self.view(self.total, unit, "all"),
                self.view(self.total, unit, "all"),
                (p.d, self.rim_z),
            ),
        }

    def start(self, unit, *lanes):
        table = self.lanes(unit)
        for lane in lanes:
            self.copy(unit, lane, *table[lane]).start()

    def wait(self, unit, *lanes):
        table = self.lanes(unit)
        for lane in lanes:
            self.copy(unit, lane, *table[lane]).wait_recv()

    def chip_sum(self, unit, add_own):
        if not 0 <= unit < len(SUM_UNITS):
            return
        w, col, width = SUM_UNITS[unit]
        self.sibling(unit, self.chip[w].at[:, :, pl.ds(col, width)]).wait_recv()
        add_own()
        self.start(unit, 1, 2, 3, 5)

    def relay(self, unit):
        if not 0 <= unit < len(SUM_UNITS):
            return
        p = self.place
        for lane, part, quarter, after in (
            (1, "a", p.quarter(1, 0), 6),
            (2, "b", p.quarter(0, 1), 4),
        ):
            self.wait(unit, lane)
            target = self.view(self.chip, unit, part, quarter)
            target[...] = (
                target[...].astype(jnp.float32)
                + self.view(self.far, unit, part)[...].astype(jnp.float32)
            ).astype(jnp.bfloat16)
            self.start(unit, after)

    def plane_sum(self, unit):
        if not 0 <= unit < len(SUM_UNITS):
            return
        mine = self.place.quarter(0, 0)
        self.wait(unit, 3, 4, 5, 6)
        total = self.view(self.chip, unit, "all", mine)[...].astype(jnp.float32)
        for side in (0, 1):
            total = total + self.view(self.near, unit, "all", side)[...].astype(jnp.float32)
        self.view(self.chip, unit, "all", mine)[...] = total.astype(jnp.bfloat16)

        @pl.when(self.is_rim)
        def _():
            self.start(unit, 7)

    def half_sum(self, unit):
        if not 0 <= unit < len(SUM_UNITS):
            return

        @pl.when(jnp.logical_not(self.is_rim))
        def _():
            self.wait(unit, 7)
            self.view(self.outer, unit, "all")[...] = (
                self.view(self.chip, unit, "all", self.place.quarter(0, 0))[...].astype(jnp.float32)
                + self.view(self.outer, unit, "all")[...].astype(jnp.float32)
            ).astype(jnp.bfloat16)
            self.start(unit, 8)

    def full_sum(self, unit):
        if not 0 <= unit < len(SUM_UNITS):
            return

        @pl.when(jnp.logical_not(self.is_rim))
        def _():
            self.wait(unit, 8)
            self.view(self.total, unit, "all")[...] = (
                self.view(self.outer, unit, "all")[...].astype(jnp.float32)
                + self.view(self.inner, unit, "all")[...].astype(jnp.float32)
            ).astype(jnp.bfloat16)
            self.start(unit, 9)

    def finish(self):
        units = range(len(SUM_UNITS))

        @pl.when(self.is_rim)
        def _():
            for unit in units:
                self.wait(unit, 9)

        for unit in units:
            table = self.lanes(unit)
            for lane in range(1, 7):
                self.copy(unit, lane, *table[lane]).wait_send()

        @pl.when(self.is_rim)
        def _():
            for unit in units:
                self.copy(unit, 7, *self.lanes(unit)[7]).wait_send()

        @pl.when(jnp.logical_not(self.is_rim))
        def _():
            for unit in units:
                for lane in (8, 9):
                    self.copy(unit, lane, *self.lanes(unit)[lane]).wait_send()


class VectorSum:
    def __init__(self, place, reduce, current, parts, send_sems, recv_sems):
        self.current, self.parts = current, parts
        self.send_sems, self.recv_sems = send_sems, recv_sems
        self.is_rim = reduce.is_rim
        self.is_core = jnp.logical_not(reduce.is_rim)
        self.peers = [place.peer(kind) for kind in "sxy"] + [
            (place.d, reduce.core_z),
            (place.d, 3 - place.z),
            (place.d, reduce.rim_z),
        ]

    def copy(self, step):
        return remote(
            self.current.at[step],
            self.parts.at[step],
            self.send_sems.at[step],
            self.recv_sems.at[step],
            self.peers[step],
        )

    def take(self, step):
        self.copy(step).wait_recv()
        self.current[step + 1] = self.current[step] + self.parts[step]

    def phase(self, number):
        if number == 0:
            self.copy(0).start()
        elif number < 3:
            self.take(number - 1)
            self.copy(number).start()
        elif number == 3:
            self.take(2)

            @pl.when(self.is_rim)
            def _():
                self.copy(3).start()

        elif number in (4, 5):

            @pl.when(self.is_core)
            def _():
                self.take(number - 1)
                self.copy(number).start()
                if number == 5:
                    self.current[6] = self.current[5]

        else:

            @pl.when(self.is_rim)
            def _():
                self.copy(5).wait_recv()
                self.current[6] = self.parts[5]
                self.copy(3).wait_send()

            for step in range(3):
                self.copy(step).wait_send()

            @pl.when(self.is_core)
            def _():
                self.copy(4).wait_send()
                self.copy(5).wait_send()


def chunk(index, size):
    return pl.ds(pl.multiple_of(index * size, size), size)


def loop(count, body):
    def step(index, carry):
        body(index)
        return carry

    lax.fori_loop(0, count, step, 0)


def fold_rows(values):
    return values[0:8] + values[8:16] + values[16:24] + values[24:32]


def layer_kernel(*refs):
    own = refs[:6]
    vectors, tokens, cotangent, block_ids = refs[6:10]
    output, gradient = refs[10:12]
    totals, vector_total = refs[12:18], refs[18]
    refs = refs[19:]
    full, refs = refs[:6], refs[6:]
    families = [refs[6 * i : 6 * (i + 1)] for i in range(5)]
    refs = refs[30:]
    (
        ring_reduce,
        ring_other,
        all_vectors,
        vecs,
        expand_shift,
        blocks,
        tangent,
        reach_t,
        queries,
        keys,
        values,
        keys_t,
        values_t,
        weights_t,
        context_t,
        context,
        first_norm,
        first_rate,
        hidden,
        hidden_t,
        active,
        active_t,
        slope,
        back_reduced,
        attended_low,
        back_context,
        back_query_t,
        back_query,
        back_key,
        spread_send,
        spread_recv,
        sums,
        expand_sum,
        current,
        parts,
    ) = refs[:35]
    (
        local_sems,
        gather_send,
        gather_recv,
        vec_send,
        vec_recv,
        tok_send,
        tok_recv,
        sum_send,
        sum_recv,
        small_send,
        small_recv,
        spread_ssem,
        spread_rsem,
    ) = refs[35:]
    back_expanded = active
    back_value = values_t
    f32, low = jnp.float32, jnp.bfloat16
    place = Place()
    gather = Gather(place, own, full, gather_send, gather_recv)
    reduce = Reduce(place, families + [totals], sum_send, sum_recv)
    small = VectorSum(place, reduce, current, parts, small_send, small_recv)
    local = [pltpu.make_async_copy(own[w], full[w].at[place.d], local_sems.at[w]) for w in range(6)]
    local.append(pltpu.make_async_copy(vectors, all_vectors.at[place.d], local_sems.at[6]))
    local.append(pltpu.make_async_copy(tokens.at[0], blocks.at[2], local_sems.at[7]))
    local.append(pltpu.make_async_copy(cotangent.at[0], tangent, local_sems.at[8]))
    for copy in local:
        copy.start()
    greet(place)

    def tick(unit):
        gather.relay(unit)
        gather.open(unit + 3)
        gather.relay_far(unit - 1)
        gather.relay_last(unit - 2)

    def vector_copy(i, shard, peer):
        return remote(vectors, all_vectors.at[shard], vec_send.at[i], vec_recv.at[i], peer)

    def token_copy(slot, source, peer_z):
        return remote(
            source, blocks.at[slot], tok_send.at[slot], tok_recv.at[slot], (place.d, peer_z)
        )

    for i, flips in enumerate(PLANE):
        vector_copy(i, place.d, (place.shard(*flips), place.z)).start()

    @pl.when(place.z < 3)
    def _():
        token_copy(1, tokens.at[0], place.z + 1).start()

    for unit in range(3):
        gather.open(unit)

    @pl.when(place.z == 0)
    def _():
        blocks[0] = jnp.zeros((TOKENS, WIDTH), low)
        blocks[1] = jnp.zeros((TOKENS, WIDTH), low)

    @pl.when(place.z == 1)
    def _():
        blocks[0] = jnp.zeros((TOKENS, WIDTH), low)

    for copy in local:
        copy.wait()

    def turn(slot):
        reach_t[:, slot * TOKENS : (slot + 1) * TOKENS] = blocks[slot].T

    turn(2)
    sums[...] = jnp.zeros_like(sums)
    tick(0)

    @pl.when(place.z > 0)
    def _():
        token_copy(1, tokens.at[0], place.z - 1).wait_recv()

        @pl.when(place.z < 3)
        def _():
            token_copy(0, blocks.at[1], place.z + 1).start()

    turn(1)
    for i, flips in enumerate(PLANE):
        vector_copy(i, place.shard(*flips), (place.shard(*flips), place.z)).wait_recv()

    def place_vectors(s, total):
        row = lax.broadcasted_iota(jnp.int32, (128, WIDTH), 0)
        lane = lax.broadcasted_iota(jnp.int32, (128, WIDTH), 1)
        pick = jnp.where((lane == row + 96 * s) & (row < 96), 1.0, 0.0).astype(low)
        return total + product(all_vectors[s], pick)

    vecs[...] = lax.fori_loop(0, 8, place_vectors, jnp.zeros((16, WIDTH), f32))
    for s in range(8):
        rows = all_vectors[s].astype(f32)
        for r in range(3):
            expand_shift[:, 384 * s + 128 * r : 384 * s + 128 * (r + 1)] = rows[8 + r : 9 + r, :]
    tick(1)

    def weight_columns(w, cols):
        return full[w][:, :, cols].reshape(8 * ROWS[w], 256)

    def project_keys(first, count):
        def body(i):
            cols = chunk(i, 256)
            source = blocks[first : first + count].reshape(count * TOKENS, WIDTH)
            part = product(source, weight_columns(KEY, cols)).astype(low)
            toks = slice(first * TOKENS, (first + count) * TOKENS)
            keys[toks, cols] = part
            keys_t[cols, toks] = part.T

        loop(3, body)

    def project_values(first, count):
        def body(i):
            cols = chunk(i, 256)
            source = blocks[first : first + count].reshape(count * TOKENS, WIDTH)
            part = (product(source, weight_columns(VALUE, cols)) + vecs[1:2, cols]).astype(low)
            toks = slice(first * TOKENS, (first + count) * TOKENS)
            values[toks, cols] = part
            values_t[cols, toks] = part.T

        loop(3, body)

    gather.arrived(0)
    project_keys(1, 2)
    tick(2)
    gather.arrived(1)
    project_values(1, 2)

    @pl.when(place.z > 1)
    def _():
        token_copy(0, blocks.at[1], place.z - 1).wait_recv()

    tick(3)
    turn(0)
    project_keys(0, 1)
    project_values(0, 1)
    gather.arrived(2)

    def project_queries(i):
        cols = chunk(i, 256)
        part = (product(blocks[2], weight_columns(QUERY, cols)) + vecs[0:1, cols]).astype(low)
        queries[:, cols] = (part.astype(f32) * HD ** (-0.5)).astype(low)

    loop(3, project_queries)

    mine = block_ids[0, place.z]
    biases = []
    for slot in range(2):
        source = place.z - 2 + slot
        seen = (source >= 0) & (block_ids[0, jnp.maximum(source, 0)] == mine)
        biases.append(jnp.where(seen, 0.0, MASKED).astype(f32))

    def half_lanes(values, half):
        lane = lax.broadcasted_iota(jnp.int32, values.shape, 1)
        keep = (lane >= 64) if half else (lane < 64)
        return jnp.where(keep, values, jnp.zeros_like(values))

    def attend(first, count):
        def body(i):
            pair = first + i
            cols = chunk(pair, 128)
            pair_queries = queries[:, cols]
            for half in range(2):
                masked = half_lanes(pair_queries, half)
                scores = [
                    right_transposed(keys[slot * TOKENS : (slot + 1) * TOKENS, cols], masked)
                    for slot in range(3)
                ]
                scores = [scores[0] + biases[0], scores[1] + biases[1], scores[2]]
                peak = jnp.maximum(
                    jnp.maximum(
                        jnp.max(scores[0], axis=0, keepdims=True),
                        jnp.max(scores[1], axis=0, keepdims=True),
                    ),
                    jnp.max(scores[2], axis=0, keepdims=True),
                )
                powers = [jnp.exp(s - peak) for s in scores]
                total = sum(jnp.sum(p, axis=0, keepdims=True) for p in powers)
                share = 1.0 / total
                for slot in range(3):
                    weights_t[2 * pair + half, slot * TOKENS : (slot + 1) * TOKENS, :] = (
                        powers[slot] * share
                    ).astype(low)
                rows = pl.ds(pl.multiple_of(pair * 128 + half * 64, 64), 64)
                context_t[rows, :] = product(values_t[rows, :], weights_t[2 * pair + half]).astype(
                    low
                )

        loop(count, body)

    attend(0, 2)
    tick(4)
    attend(2, 2)
    tick(5)
    attend(4, 2)
    gather.arrived(3)

    def project_output(i):
        cols = chunk(i, 256)
        if True:
            part = product(context[...], weight_columns(OUT, cols)) + vecs[2:3, cols]
        gradient[:, cols] = part + blocks[2, :, cols].astype(f32)

    context[...] = context_t[...].T
    loop(3, project_output)

    def mean(values):
        return jnp.sum(values, axis=-1, keepdims=True) * (1.0 / WIDTH)

    def first_normalise(i):
        rows = chunk(i, 32)
        values = gradient[rows, :]
        centred = values - mean(values)
        rate = lax.rsqrt(mean(centred * centred) + EPSILON)
        norm = centred * rate
        first_norm[rows, :] = norm
        first_rate[rows, :] = jnp.broadcast_to(rate, (32, 128))
        hidden[rows, :] = (norm * vecs[3:4, :] + vecs[4:5, :]).astype(low)

    loop(8, first_normalise)
    hidden_t[...] = hidden[...].T
    tick(6)

    def expand(unit):
        def body(i):
            cols = chunk(3 * unit + i, 256)
            inner = product(hidden[...], weight_columns(EXPAND, cols)) + expand_shift[:, cols]
            share = 0.5 * (1.0 + lax.erf(inner * 0.7071067811865476))
            bell = jnp.exp(inner * inner * -0.5) * 0.3989422804014327
            act = (inner * share).astype(low)
            active[:, cols] = act
            active_t[cols, :] = act.T
            slope[:, cols] = (share + inner * bell).astype(low)

        loop(3, body)

    for j in range(4):
        gather.arrived(4 + j)
        expand(j)
        tick(7 + j)

    for j in range(3):
        if j:
            tick(10 + j)
        gather.arrived(8 + j)
        cols = slice(256 * j, 256 * (j + 1))
        part = product(active[...], full[REDUCE][:, :, cols].reshape(3072, 256))
        gradient[:, cols] = part + vecs[5:6, cols] + hidden[:, cols].astype(f32)

    def last_normalise(i):
        rows = chunk(i, 32)
        values = gradient[rows, :]
        centred = values - mean(values)
        rate = lax.rsqrt(mean(centred * centred) + EPSILON)
        norm = centred * rate
        output[rows, :] = (norm * vecs[6:7, :] + vecs[7:8, :]).astype(low)
        arriving = tangent[rows, :].astype(f32)
        sums[0] += fold_rows(arriving * norm)
        sums[1] += fold_rows(arriving)
        scaled = arriving * vecs[6:7, :]
        back = (scaled - mean(scaled) - norm * mean(scaled * norm)) * rate
        gradient[rows, :] = back
        rounded = back.astype(low)
        back_reduced[rows, :] = rounded
        sums[2] += fold_rows(rounded.astype(f32))

    loop(8, last_normalise)

    def shard_rows(shard, count):
        return pl.ds(pl.multiple_of(shard * count, 32), count)

    def group(source, parity, toks=None):
        picks = []
        for quarter in range(4):
            rows = shard_rows(2 * quarter + parity, 96)
            picks.append(source[rows, :] if toks is None else source[rows, toks])
        return jnp.concatenate(picks, axis=0)

    def terms(unit, parity, put):
        w, col, width = SUM_UNITS[unit]
        if w == REDUCE:

            def body(quarter):
                rows = shard_rows(2 * quarter + parity, 384)
                put(
                    quarter,
                    slice(0, 256),
                    product(active_t[rows, :], back_reduced[:, col : col + 256]),
                )

            loop(4, body)
            return

        if w == EXPAND:
            lhs = lambda: group(hidden_t, parity)
            rhs = lambda i: back_expanded[:, chunk(col // 256 + i, 256)]
        elif w == OUT:
            lhs = lambda: group(context_t, parity)
            rhs = lambda i: attended_low[:, chunk(i, 256)]
        elif w == QUERY:
            lhs = lambda: group(reach_t, parity, slice(512, 768))
            rhs = lambda i: back_query[:, chunk(i, 256)]
        elif w == KEY:
            lhs = lambda: group(reach_t, parity)
            rhs = lambda i: back_key[:, chunk(i, 256)]
        else:
            lhs = lambda: group(reach_t, parity)
            rhs = lambda i: back_value[:, chunk(i, 256)]

        def body(i):
            term = product(lhs(), rhs(i))
            for quarter in range(4):
                put(quarter, chunk(i, 256), term[96 * quarter : 96 * (quarter + 1)])

        loop(3, body)

    def slot_of(unit):
        return ring_reduce.at[unit % 2] if unit < 3 else ring_other.at[(unit - 3) % 3]

    def ring_before(unit):
        return unit - 2 if unit == 2 else (unit - 3 if unit >= 6 else None)

    def send_half(unit):
        if unit >= len(SUM_UNITS):
            return
        slot = slot_of(unit)
        earlier = ring_before(unit)
        if earlier is not None:
            reduce.sibling(earlier, slot).wait_send()

        def put(quarter, cols, term):
            slot[quarter, :, cols] = term.astype(low)

        terms(unit, 1 - place.c, put)
        reduce.sibling(unit, slot).start()

    def own_half(unit):
        if unit >= len(SUM_UNITS):
            return
        w, col, width = SUM_UNITS[unit]

        def add_own():
            def put(quarter, cols, term):
                if w == REDUCE:
                    where = (quarter, slice(None), slice(col, col + 256))
                elif w == EXPAND:
                    where = (quarter, slice(None), pl.ds(pl.multiple_of(cols.start + col, 256), 256))
                else:
                    where = (quarter, slice(None), cols)
                reduce.chip[w][where] = (term + reduce.chip[w][where].astype(f32)).astype(low)

            terms(unit, place.c, put)

        reduce.chip_sum(unit, add_own)

    def step(unit):
        own_half(unit)
        reduce.relay(unit - 1)
        reduce.plane_sum(unit - 2)
        reduce.half_sum(unit - 3)
        reduce.full_sum(unit - 4)

    def back_expand(j):
        def body(i):
            shard = 2 * j + i
            cols = pl.ds(pl.multiple_of(shard * 384, 128), 384)
            back = right_transposed(back_reduced[...], full[REDUCE][shard])
            rounded = (back * slope[:, cols].astype(f32)).astype(low)
            back_expanded[:, cols] = rounded
            expand_sum[:, cols] = jnp.sum(rounded.astype(f32), axis=0, keepdims=True)

        loop(2, body)

        def gather_hidden(i):
            cols = slice(768 * j, 768 * (j + 1))
            rows = full[EXPAND][pl.ds(4 * i, 4), :, cols].reshape(384, 768)
            out = pl.ds(pl.multiple_of(i * 384, 128), 384)
            gradient[:, out] += right_transposed(back_expanded[:, cols], rows)

        loop(2, gather_hidden)

    send_half(0)
    send_half(1)
    step(0)
    back_expand(0)
    send_half(2)
    step(1)
    back_expand(1)
    send_half(3)
    step(2)
    back_expand(2)
    send_half(4)
    step(3)
    back_expand(3)
    send_half(5)
    step(4)

    def first_back(i):
        rows = chunk(i, 32)
        back = gradient[rows, :]
        norm = first_norm[rows, :]
        sums[3] += fold_rows(back * norm)
        sums[4] += fold_rows(back)
        scaled = back * vecs[3:4, :]
        rate = first_rate[rows, 0:1]
        back = (scaled - mean(scaled) - norm * mean(scaled * norm)) * rate
        gradient[rows, :] = back
        rounded = back.astype(low)
        attended_low[rows, :] = rounded
        sums[5] += fold_rows(rounded.astype(f32))

    loop(8, first_back)

    def weight_rows(w, i):
        return full[w][pl.ds(4 * i, 4), :, :].reshape(384, WIDTH)

    def back_output(i):
        out = pl.ds(pl.multiple_of(i * 384, 128), 384)
        back_context[:, out] = right_transposed(attended_low[...], weight_rows(OUT, i)).astype(low)

    loop(2, back_output)
    send_half(6)
    step(5)

    def attend_back(first, count):
        def body(i):
            pair = first + i
            cols = chunk(pair, 128)
            pair_back = back_context[:, cols]
            pair_queries = queries[:, cols]
            key_term, value_term = 0.0, 0.0
            for half in range(2):
                masked = half_lanes(pair_back, half)
                weights = weights_t[2 * pair + half].astype(f32)
                back = right_transposed(values[:, cols], masked)
                inner = jnp.sum(weights * back, axis=0, keepdims=True)
                back_scores = (weights * (back - inner)).astype(low)
                key_term += product(back_scores, half_lanes(pair_queries, half))
                value_term += product(weights_t[2 * pair + half], masked)
                rows = pl.ds(pl.multiple_of(pair * 128 + half * 64, 64), 64)
                back_query_t[rows, :] = (
                    product(keys_t[rows, :], back_scores) * HD ** (-0.5)
                ).astype(low)
            back_key[:, cols] = key_term.astype(low)
            back_value[:, cols] = value_term.astype(low)

        loop(count, body)

    attend_back(0, 3)
    send_half(7)
    step(6)
    attend_back(3, 3)
    back_query[...] = back_query_t[...].T
    send_half(8)
    step(7)

    def spread_copy(slot):
        return remote(
            spread_send.at[slot],
            spread_recv.at[slot],
            spread_ssem.at[slot],
            spread_rsem.at[slot],
            (place.d, place.z - 1),
        )

    def spread_into(block):
        toks = slice(block * TOKENS, (block + 1) * TOKENS)

        def body(i):
            out = pl.ds(pl.multiple_of(i * 384, 128), 384)
            part = right_transposed(back_key[toks, :], weight_rows(KEY, i)) + right_transposed(
                back_value[toks, :], weight_rows(VALUE, i)
            )
            if block == 2:
                part = part + right_transposed(back_query[...], weight_rows(QUERY, i))
                gradient[:, out] += part
            else:
                spread_send[block, :, out] = part.astype(low)

        loop(2, body)

    spread_into(0)

    @pl.when(place.z > 1)
    def _():
        spread_copy(0).start()

    spread_into(1)

    @pl.when(place.z == 3)
    def _():
        spread_copy(1).start()

    def column_total(values):
        return jnp.sum(values, axis=0, keepdims=True)

    rows = [
        column_total(back_query[...].astype(f32)),
        column_total(back_value[...].astype(f32)),
        column_total(sums[5]),
        column_total(sums[3]),
        column_total(sums[4]),
        column_total(sums[2]),
        column_total(sums[0]),
        column_total(sums[1]),
    ] + [expand_sum[:, WIDTH * i : WIDTH * (i + 1)] for i in range(4)]
    for i, row in enumerate(rows):
        current[0, i : i + 1, :] = row
    current[0, 12:16, :] = jnp.zeros((4, WIDTH), f32)
    small.phase(0)
    send_half(9)
    step(8)
    small.phase(1)

    @pl.when((place.z > 0) & (place.z < 3))
    def _():
        pltpu_copy = remote(
            spread_send.at[0],
            spread_recv.at[0],
            spread_ssem.at[0],
            spread_rsem.at[0],
            (place.d, place.z + 1),
        )
        pltpu_copy.wait_recv()
        spread_send[1] = (spread_send[1].astype(f32) + spread_recv[0].astype(f32)).astype(low)
        spread_copy(1).start()

    spread_into(2)
    send_half(10)
    step(9)
    small.phase(2)
    step(10)
    small.phase(3)
    step(11)
    small.phase(4)
    step(12)
    small.phase(5)
    step(13)

    @pl.when(place.z < 3)
    def _():
        remote(
            spread_send.at[1],
            spread_recv.at[1],
            spread_ssem.at[1],
            spread_rsem.at[1],
            (place.d, place.z + 1),
        ).wait_recv()

        def body(i):
            rows = chunk(i, 32)
            gradient[rows, :] += spread_recv[1, rows, :].astype(f32)

        loop(8, body)

    step(14)
    small.phase(6)
    vector_total[...] = current[6]

    gather.drain()
    for i, flips in enumerate(PLANE):
        vector_copy(i, place.d, (place.shard(*flips), place.z)).wait_send()

    @pl.when(place.z < 3)
    def _():
        token_copy(1, tokens.at[0], place.z + 1).wait_send()

    @pl.when((place.z > 0) & (place.z < 3))
    def _():
        token_copy(0, blocks.at[1], place.z + 1).wait_send()

    @pl.when(place.z > 1)
    def _():
        spread_copy(0).wait_send()

    @pl.when(place.z > 0)
    def _():
        spread_copy(1).wait_send()

    waited = [ring_before(unit) for unit in range(len(SUM_UNITS))]
    for unit in range(len(SUM_UNITS)):
        if unit not in waited:
            reduce.sibling(unit, slot_of(unit)).wait_send()
    reduce.finish()


def layer_call(weights, vectors, tokens, cotangent, block_ids):
    hbm = pl.BlockSpec(memory_space=pl.ANY)
    vmem = pl.BlockSpec(memory_space=pltpu.VMEM)
    dma = pltpu.SemaphoreType.DMA
    low, f32 = jnp.bfloat16, jnp.float32
    gathers, units = len(GATHER_UNITS), len(SUM_UNITS)

    def family(*lead):
        return [pltpu.VMEM((*lead, ROWS[w], COLS[w]), low) for w in range(6)]

    def wide(rows, cols, kind=low):
        return pltpu.VMEM((rows, cols), kind)

    scratch = (
        family(8)
        + family(4)
        + family()
        + family(2)
        + family()
        + family()
        + [
            pltpu.VMEM((2, 4, 384, 256), low),
            pltpu.VMEM((3, 4, 96, WIDTH), low),
            pltpu.VMEM((8, 16, 128), low),
            wide(16, WIDTH, f32),
            wide(1, 3072, f32),
            pltpu.VMEM((3, TOKENS, WIDTH), low),
            wide(TOKENS, WIDTH),
            wide(WIDTH, 3 * TOKENS),
            wide(TOKENS, WIDTH),
            wide(3 * TOKENS, WIDTH),
            wide(3 * TOKENS, WIDTH),
            wide(WIDTH, 3 * TOKENS),
            wide(WIDTH, 3 * TOKENS),
            pltpu.VMEM((12, 3 * TOKENS, TOKENS), low),
            wide(WIDTH, TOKENS),
            wide(TOKENS, WIDTH),
            wide(TOKENS, WIDTH, f32),
            wide(TOKENS, 128, f32),
            wide(TOKENS, WIDTH),
            wide(WIDTH, TOKENS),
            wide(TOKENS, 3072),
            wide(3072, TOKENS),
            wide(TOKENS, 3072),
            wide(TOKENS, WIDTH),
            wide(TOKENS, WIDTH),
            wide(TOKENS, WIDTH),
            wide(WIDTH, TOKENS),
            wide(TOKENS, WIDTH),
            wide(3 * TOKENS, WIDTH),
            pltpu.VMEM((2, TOKENS, WIDTH), low),
            pltpu.VMEM((2, TOKENS, WIDTH), low),
            pltpu.VMEM((6, 8, WIDTH), f32),
            wide(1, 3072, f32),
            pltpu.VMEM((7, 16, WIDTH), f32),
            pltpu.VMEM((6, 16, WIDTH), f32),
            dma((9,)),
            dma((gathers, 14)),
            dma((gathers, 14)),
            dma((7,)),
            dma((7,)),
            dma((2,)),
            dma((2,)),
            dma((units, 10)),
            dma((units, 10)),
            dma((6,)),
            dma((6,)),
            dma((2,)),
            dma((2,)),
        ]
    )
    return pl.pallas_call(
        layer_kernel,
        out_shape=[
            jax.ShapeDtypeStruct((TOKENS, WIDTH), low),
            jax.ShapeDtypeStruct((TOKENS, WIDTH), f32),
        ]
        + [jax.ShapeDtypeStruct((ROWS[w], COLS[w]), low) for w in range(6)]
        + [jax.ShapeDtypeStruct((16, WIDTH), f32)],
        in_specs=[hbm] * 9 + [pl.BlockSpec(memory_space=pltpu.SMEM)],
        out_specs=[vmem] * 9,
        scratch_shapes=scratch,
        compiler_params=pltpu.CompilerParams(
            collective_id=0, has_side_effects=True, vmem_limit_bytes=67043328
        ),
        name="layer",
    )(*weights, vectors, tokens, cotangent, block_ids)


def fitted_shards(
    inputs,
    block_ids,
    query_weight,
    query_bias,
    key_weight,
    value_weight,
    value_bias,
    output_weight,
    output_bias,
    attention_gain,
    attention_shift,
    expand_weight,
    expand_bias,
    reduce_weight,
    reduce_bias,
    final_gain,
    final_shift,
    cotangent,
):
    low = jnp.bfloat16
    small = [
        query_bias,
        value_bias,
        output_bias,
        attention_gain,
        attention_shift,
        reduce_bias,
        final_gain,
        final_shift,
    ]
    packed = jnp.concatenate(
        [
            jnp.pad(jnp.stack(small), ((0, 0), (0, 32))),
            expand_bias.reshape(3, 128),
            jnp.zeros((5, 128), low),
        ]
    )
    output, gradient, *totals, vector_total = layer_call(
        (key_weight, value_weight, query_weight, output_weight, expand_weight, reduce_weight),
        packed,
        inputs,
        cotangent,
        block_ids,
    )
    key_sum, value_sum, query_sum, output_sum, expand_sum, reduce_sum = (
        t.astype(jnp.float32) for t in totals
    )
    d = lax.axis_index("dp")
    small_sums = lax.dynamic_slice(vector_total[:8], (0, 96 * d), (8, 96))
    expand_part = lax.dynamic_slice(vector_total[8:12].reshape(3072), (384 * d,), (384,))
    return (
        output[None],
        gradient[None],
        query_sum,
        small_sums[0],
        key_sum,
        value_sum,
        small_sums[1],
        output_sum,
        small_sums[2],
        small_sums[3],
        small_sums[4],
        expand_sum,
        expand_part,
        reduce_sum,
        small_sums[5],
        small_sums[6],
        small_sums[7],
    )


def solution(mesh):
    placed = (
        P("dp", "seq", None),
        P("dp", None),
        P("dp", None),
        P("dp"),
        P("dp", None),
        P("dp", None),
        P("dp"),
        P("dp", None),
        P("dp"),
        P("dp"),
        P("dp"),
        P("dp", None),
        P("dp"),
        P("dp", None),
        P("dp"),
        P("dp"),
        P("dp"),
        P("dp", "seq", None),
    )
    fitted = mesh.shape["dp"] == 8 and mesh.shape["seq"] == 4
    return jax.shard_map(
        fitted_shards if fitted else general_shards,
        mesh=mesh,
        in_specs=placed,
        out_specs=(
            P("dp", "seq", None),
            P("dp", "seq", None),
            P("dp", None),
            P("dp"),
            P("dp", None),
            P("dp", None),
            P("dp"),
            P("dp", None),
            P("dp"),
            P("dp"),
            P("dp"),
            P("dp", None),
            P("dp"),
            P("dp", None),
            P("dp"),
            P("dp"),
            P("dp"),
        ),
        check_vma=False,
    )
```

profile of v0, /device:TPU:0, one launch (start us, length us, event | category | flops | bytes accessed | tf_op | source)
XLA Modules:
  0.0 185.2 jit_solution(653110530566830851)
XLA Ops:
  0.7 0.8 stack.35
  1.5 0.1 pad.7.clone
  1.5 1.3 fusion.2.refs_6_
  2.9 171.6 %layer.1 = (bf16[256,768]{1,0:T(8,128)(2,1)}, f32[256,768]{1,0:T(8,128)}, bf16[96,768]{1,0:T(8,128)(2,1)}, bf16[96,768]{1,0:T(8,128)(2,1)}, bf16[96,768]{1,0:T(8...) custom-call(bf16[96,768]{1,0:T(8,128)(2,1)} %refs_0_.1, ...), custom_call_target="tpu_custom_call" | custom-call | tf_op jit(solution)/shard_map/layer/pallas_call | solution.py:1467
  174.4 0.0 copy-start.1
  174.5 0.8 slice.30
  175.3 0.1 constant_dynamic-slice_fusion
  175.3 0.5 slice_bitcast_fusion
  175.9 0.7 slice.36
  176.6 0.7 dynamic_slice.7
  177.3 2.2 %convert_element_type.24 = f32[96,3072]{1,0:T(8,128)} convert(bf16[96,3072]{1,0:T(8,128)(2,1)} %get-tuple-element.33) | non-fusion elementwise | flops 294912 | bytes 1769472 | tf_op jit(solution)/shard_map/convert_element_type | solution.py:1531
  179.5 0.0 copy-start.6
  179.5 0.0 copy-start.5
  179.5 0.0 copy-done.1
  179.5 0.0 copy-start.4
  179.5 0.0 copy-start.3
  179.5 1.1 convert_element_type.25
  180.6 0.0 copy-start.2
  180.6 0.0 copy-done.6
  180.6 0.0 copy-start
  180.6 0.7 convert_element_type.20
  181.3 0.0 copy-done.5
  181.3 0.7 convert_element_type.21
  182.1 0.0 copy-done.4
  182.1 0.7 convert_element_type.22
  182.8 0.0 copy-done.3
  182.8 0.7 convert_element_type.23
  183.5 0.0 copy-done.2
  183.5 0.7 copy.37
  184.3 0.0 copy-done
  184.3 0.9 copy.38
  (2 shorter events, 0.0 us)
Async XLA Ops:
  174.4 5.0 %copy-start.1 = (bf16[384,768]{1,0:T(8,128)(2,1)S(1)}, bf16[384,768]{1,0:T(8,128)(2,1)}, u32[]{:S(2)}) copy-start(bf16[384,768]{1,0:T(8,128)(2,1)} %get-tuple-element.34) | copy-start | bytes 1769476
  179.5 1.1 copy-start.6
  179.5 1.9 %copy-start.5 = (bf16[96,768]{1,0:T(8,128)(2,1)S(1)}, bf16[96,768]{1,0:T(8,128)(2,1)}, u32[]{:S(2)}) copy-start(bf16[96,768]{1,0:T(8,128)(2,1)} %get-tuple-element.30) | copy-start | bytes 442372
  179.5 2.6 %copy-start.4 = (bf16[96,768]{1,0:T(8,128)(2,1)S(1)}, bf16[96,768]{1,0:T(8,128)(2,1)}, u32[]{:S(2)}) copy-start(bf16[96,768]{1,0:T(8,128)(2,1)} %get-tuple-element.31) | copy-start | bytes 442372
  179.5 3.3 %copy-start.3 = (bf16[96,768]{1,0:T(8,128)(2,1)S(1)}, bf16[96,768]{1,0:T(8,128)(2,1)}, u32[]{:S(2)}) copy-start(bf16[96,768]{1,0:T(8,128)(2,1)} %get-tuple-element.32) | copy-start | bytes 442372
  180.6 3.0 %copy-start.2 = (bf16[256,768]{1,0:T(8,128)(2,1)S(1)}, bf16[256,768]{1,0:T(8,128)(2,1)}, u32[]{:S(2)}) copy-start(bf16[256,768]{1,0:T(8,128)(2,1)} %get-tuple-element.26) | copy-start | bytes 1179652
  180.6 3.7 %copy-start = (f32[256,768]{1,0:T(8,128)S(1)}, f32[256,768]{1,0:T(8,128)}, u32[]{:S(2)}) copy-start(f32[256,768]{1,0:T(8,128)} %get-tuple-element.27) | copy-start | bytes 2359300
where the time goes:
time: 185 us
  Pallas kernels  172 us (93%)
  other arithmetic  7.55 us (4%)
  local copies, waits for them, and re-layouts  5.35 us (3%)
    pallas_call x1, Pallas kernels, layer_call(): pl.pallas_call(layer_kernel, out_shape=[jax.ShapeDtypeStruct((TOKENS, WID...  172 us
    convert_element_type x6, other arithmetic, fitted_shards(): t.astype(jnp.float32)  6.2 us

commit v1 on v0

--- a/solution.py
+++ b/solution.py
@@ -529,8 +529,8 @@
 
 
 class Reduce:
-    def __init__(self, place, buffers, send_sems, recv_sems):
-        self.place = place
+    def __init__(self, place, buffers, out, send_sems, recv_sems, out_sems):
+        self.place, self.out, self.out_sems = place, out, out_sems
         self.chip, self.far, self.near, self.outer, self.inner, self.total = buffers
         self.send_sems, self.recv_sems = send_sems, recv_sems
         self.rim_z = jnp.where(place.z < 2, 0, 3)
@@ -655,15 +655,26 @@
             ).astype(jnp.bfloat16)
             self.start(unit, 9)
 
+    def result(self, unit):
+        return pltpu.make_async_copy(
+            self.view(self.total, unit, "all"), self.view(self.out, unit, "all"), self.out_sems.at[unit]
+        )
+
+    def collect(self, unit):
+        if not 0 <= unit < len(SUM_UNITS):
+            return
+
+        @pl.when(self.is_rim)
+        def _():
+            self.wait(unit, 9)
+
+        self.result(unit).start()
+
     def finish(self):
         units = range(len(SUM_UNITS))
 
-        @pl.when(self.is_rim)
-        def _():
-            for unit in units:
-                self.wait(unit, 9)
-
         for unit in units:
+            self.result(unit).wait()
             table = self.lanes(unit)
             for lane in range(1, 7):
                 self.copy(unit, lane, *table[lane]).wait_send()
@@ -763,12 +774,12 @@
 def layer_kernel(*refs):
     own = refs[:6]
     vectors, tokens, cotangent, block_ids = refs[6:10]
-    output, gradient = refs[10:12]
-    totals, vector_total = refs[12:18], refs[18]
+    output_hbm, gradient_hbm = refs[10:12]
+    totals_hbm, vector_total = refs[12:18], refs[18]
     refs = refs[19:]
     full, refs = refs[:6], refs[6:]
-    families = [refs[6 * i : 6 * (i + 1)] for i in range(5)]
-    refs = refs[30:]
+    families = [refs[6 * i : 6 * (i + 1)] for i in range(6)]
+    refs = refs[36:]
     (
         ring_reduce,
         ring_other,
@@ -805,7 +816,9 @@
         expand_sum,
         current,
         parts,
-    ) = refs[:35]
+        output,
+        gradient,
+    ) = refs[:37]
     (
         local_sems,
         gather_send,
@@ -820,13 +833,16 @@
         small_recv,
         spread_ssem,
         spread_rsem,
-    ) = refs[35:]
+        out_sems,
+    ) = refs[37:]
     back_expanded = active
     back_value = values_t
     f32, low = jnp.float32, jnp.bfloat16
     place = Place()
     gather = Gather(place, own, full, gather_send, gather_recv)
-    reduce = Reduce(place, families + [totals], sum_send, sum_recv)
+    reduce = Reduce(place, families, totals_hbm, sum_send, sum_recv, out_sems)
+    output_copy = pltpu.make_async_copy(output, output_hbm, local_sems.at[9])
+    gradient_copy = pltpu.make_async_copy(gradient, gradient_hbm, local_sems.at[10])
     small = VectorSum(place, reduce, current, parts, small_send, small_recv)
     local = [pltpu.make_async_copy(own[w], full[w].at[place.d], local_sems.at[w]) for w in range(6)]
     local.append(pltpu.make_async_copy(vectors, all_vectors.at[place.d], local_sems.at[6]))
@@ -838,7 +854,7 @@
 
     def tick(unit):
         gather.relay(unit)
-        gather.open(unit + 3)
+        gather.open(unit + 2)
         gather.relay_far(unit - 1)
         gather.relay_last(unit - 2)
 
@@ -857,7 +873,7 @@
     def _():
         token_copy(1, tokens.at[0], place.z + 1).start()
 
-    for unit in range(3):
+    for unit in range(2):
         gather.open(unit)
 
     @pl.when(place.z == 0)
@@ -1074,6 +1090,7 @@
         sums[2] += fold_rows(rounded.astype(f32))
 
     loop(8, last_normalise)
+    output_copy.start()
 
     def shard_rows(shard, count):
         return pl.ds(pl.multiple_of(shard * count, 32), count)
@@ -1087,44 +1104,36 @@
 
     def terms(unit, parity, put):
         w, col, width = SUM_UNITS[unit]
+        first = col // 256
         if w == REDUCE:
 
             def body(quarter):
                 rows = shard_rows(2 * quarter + parity, 384)
-                put(
-                    quarter,
-                    slice(0, 256),
-                    product(active_t[rows, :], back_reduced[:, col : col + 256]),
-                )
+                put(quarter, 0, product(active_t[rows, :], back_reduced[:, col : col + 256]))
 
             loop(4, body)
             return
 
         if w == EXPAND:
-            lhs = lambda: group(hidden_t, parity)
-            rhs = lambda i: back_expanded[:, chunk(col // 256 + i, 256)]
+            lhs, rhs = (lambda: group(hidden_t, parity)), back_expanded
         elif w == OUT:
-            lhs = lambda: group(context_t, parity)
-            rhs = lambda i: attended_low[:, chunk(i, 256)]
+            lhs, rhs = (lambda: group(context_t, parity)), attended_low
         elif w == QUERY:
-            lhs = lambda: group(reach_t, parity, slice(512, 768))
-            rhs = lambda i: back_query[:, chunk(i, 256)]
-        elif w == KEY:
-            lhs = lambda: group(reach_t, parity)
-            rhs = lambda i: back_key[:, chunk(i, 256)]
+            lhs, rhs = (lambda: group(reach_t, parity, slice(512, 768))), back_query
         else:
-            lhs = lambda: group(reach_t, parity)
-            rhs = lambda i: back_value[:, chunk(i, 256)]
+            lhs, rhs = (lambda: group(reach_t, parity)), back_key if w == KEY else back_value
 
         def body(i):
-            term = product(lhs(), rhs(i))
+            term = product(lhs(), rhs[:, chunk(first + i, 256)])
             for quarter in range(4):
-                put(quarter, chunk(i, 256), term[96 * quarter : 96 * (quarter + 1)])
-
-        loop(3, body)
+                put(quarter, i, term[96 * quarter : 96 * (quarter + 1)])
+
+        loop(width // 256, body)
 
     def slot_of(unit):
-        return ring_reduce.at[unit % 2] if unit < 3 else ring_other.at[(unit - 3) % 3]
+        if unit < 3:
+            return ring_reduce.at[unit % 2]
+        return ring_other.at[(unit - 3) % 3, :, :, pl.ds(0, SUM_UNITS[unit][2])]
 
     def ring_before(unit):
         return unit - 2 if unit == 2 else (unit - 3 if unit >= 6 else None)
@@ -1132,16 +1141,16 @@
     def send_half(unit):
         if unit >= len(SUM_UNITS):
             return
-        slot = slot_of(unit)
         earlier = ring_before(unit)
         if earlier is not None:
-            reduce.sibling(earlier, slot).wait_send()
-
-        def put(quarter, cols, term):
-            slot[quarter, :, cols] = term.astype(low)
+            reduce.sibling(earlier, slot_of(earlier)).wait_send()
+        ring = ring_reduce.at[unit % 2] if unit < 3 else ring_other.at[(unit - 3) % 3]
+
+        def put(quarter, i, term):
+            ring[quarter, :, chunk(i, 256)] = term.astype(low)
 
         terms(unit, 1 - place.c, put)
-        reduce.sibling(unit, slot).start()
+        reduce.sibling(unit, slot_of(unit)).start()
 
     def own_half(unit):
         if unit >= len(SUM_UNITS):
@@ -1149,13 +1158,8 @@
         w, col, width = SUM_UNITS[unit]
 
         def add_own():
-            def put(quarter, cols, term):
-                if w == REDUCE:
-                    where = (quarter, slice(None), slice(col, col + 256))
-                elif w == EXPAND:
-                    where = (quarter, slice(None), pl.ds(pl.multiple_of(cols.start + col, 256), 256))
-                else:
-                    where = (quarter, slice(None), cols)
+            def put(quarter, i, term):
+                where = (quarter, slice(None), chunk(col // 256 + i, 256))
                 reduce.chip[w][where] = (term + reduce.chip[w][where].astype(f32)).astype(low)
 
             terms(unit, place.c, put)
@@ -1168,6 +1172,7 @@
         reduce.plane_sum(unit - 2)
         reduce.half_sum(unit - 3)
         reduce.full_sum(unit - 4)
+        reduce.collect(unit - 7)
 
     def back_expand(j):
         def body(i):
@@ -1340,6 +1345,7 @@
     small.phase(2)
     step(10)
     small.phase(3)
+    send_half(12)
     step(11)
     small.phase(4)
     step(12)
@@ -1362,8 +1368,14 @@
 
         loop(8, body)
 
+    gradient_copy.start()
     step(14)
+    step(15)
+    step(16)
     small.phase(6)
+    step(17)
+    step(18)
+    step(19)
     vector_total[...] = current[6]
 
     gather.drain()
@@ -1391,6 +1403,8 @@
         if unit not in waited:
             reduce.sibling(unit, slot_of(unit)).wait_send()
     reduce.finish()
+    output_copy.wait()
+    gradient_copy.wait()
 
 
 def layer_call(weights, vectors, tokens, cotangent, block_ids):
@@ -1411,6 +1425,7 @@
         + family(4)
         + family()
         + family(2)
+        + family()
         + family()
         + family()
         + [
@@ -1449,7 +1464,9 @@
             wide(1, 3072, f32),
             pltpu.VMEM((7, 16, WIDTH), f32),
             pltpu.VMEM((6, 16, WIDTH), f32),
-            dma((9,)),
+            wide(TOKENS, WIDTH),
+            wide(TOKENS, WIDTH, f32),
+            dma((11,)),
             dma((gathers, 14)),
             dma((gathers, 14)),
             dma((7,)),
@@ -1462,6 +1479,7 @@
             dma((6,)),
             dma((2,)),
             dma((2,)),
+            dma((units,)),
         ]
     )
     return pl.pallas_call(
@@ -1473,13 +1491,65 @@
         + [jax.ShapeDtypeStruct((ROWS[w], COLS[w]), low) for w in range(6)]
         + [jax.ShapeDtypeStruct((16, WIDTH), f32)],
         in_specs=[hbm] * 9 + [pl.BlockSpec(memory_space=pltpu.SMEM)],
-        out_specs=[vmem] * 9,
+        out_specs=[hbm] * 8 + [vmem],
         scratch_shapes=scratch,
         compiler_params=pltpu.CompilerParams(
             collective_id=0, has_side_effects=True, vmem_limit_bytes=67043328
         ),
         name="layer",
     )(*weights, vectors, tokens, cotangent, block_ids)
+
+
+def finish_kernel(*refs):
+    passed, sums, vectors = refs[:2], refs[2:8], refs[8]
+    passed_out, sums_out, small_out, expand_out = refs[9:11], refs[11:17], refs[17:25], refs[25]
+    passed_buf, sums_buf, wide_buf = refs[26:28], refs[28:34], refs[34:40]
+    in_sems, out_sems = refs[40:]
+    order = [REDUCE, EXPAND, OUT, QUERY, KEY, VALUE]
+    loads = [pltpu.make_async_copy(sums[w], sums_buf[w], in_sems.at[w]) for w in range(6)]
+    stores = [pltpu.make_async_copy(wide_buf[w], sums_out[w], out_sems.at[w]) for w in range(6)]
+    for i in range(2):
+        loads.append(pltpu.make_async_copy(passed[i], passed_buf[i], in_sems.at[6 + i]))
+        stores.append(pltpu.make_async_copy(passed_buf[i], passed_out[i], out_sems.at[6 + i]))
+    for w in order + [6, 7]:
+        loads[w].start()
+    d = lax.axis_index("dp")
+    turned = pltpu.roll(vectors[0:8, :], lax.rem(WIDTH - 96 * d, WIDTH), 1)
+    for i in range(8):
+        small_out[i][...] = turned[i, 0:96]
+    expand_row = vectors[pl.ds(8 + d // 2, 1), pl.ds(pl.multiple_of(384 * (d % 2), 128), 384)]
+    expand_out[...] = expand_row[0]
+    for w in order:
+        loads[w].wait()
+        wide_buf[w][...] = sums_buf[w][...].astype(jnp.float32)
+        stores[w].start()
+    for i in (6, 7):
+        loads[i].wait()
+        stores[i].start()
+    for store in stores:
+        store.wait()
+
+
+def finish_call(output, gradient, totals, vectors):
+    hbm = pl.BlockSpec(memory_space=pl.ANY)
+    vmem = pl.BlockSpec(memory_space=pltpu.VMEM)
+    low, f32 = jnp.bfloat16, jnp.float32
+    passed = [jax.ShapeDtypeStruct((TOKENS, WIDTH), kind) for kind in (low, f32)]
+    sums = [jax.ShapeDtypeStruct((ROWS[w], COLS[w]), f32) for w in range(6)]
+    return pl.pallas_call(
+        finish_kernel,
+        out_shape=passed
+        + sums
+        + [jax.ShapeDtypeStruct((96,), f32)] * 8
+        + [jax.ShapeDtypeStruct((384,), f32)],
+        in_specs=[hbm] * 8 + [vmem],
+        out_specs=[hbm] * 8 + [vmem] * 9,
+        scratch_shapes=[pltpu.VMEM(s.shape, s.dtype) for s in passed]
+        + [pltpu.VMEM(s.shape, low) for s in sums]
+        + [pltpu.VMEM(s.shape, f32) for s in sums]
+        + [pltpu.SemaphoreType.DMA((8,))] * 2,
+        name="finish",
+    )(output, gradient, *totals, vectors)
 
 
 def fitted_shards(
@@ -1527,12 +1597,10 @@
         cotangent,
         block_ids,
     )
-    key_sum, value_sum, query_sum, output_sum, expand_sum, reduce_sum = (
-        t.astype(jnp.float32) for t in totals
-    )
-    d = lax.axis_index("dp")
-    small_sums = lax.dynamic_slice(vector_total[:8], (0, 96 * d), (8, 96))
-    expand_part = lax.dynamic_slice(vector_total[8:12].reshape(3072), (384 * d,), (384,))
+    done = finish_call(output, gradient, totals, vector_total)
+    output, gradient = done[:2]
+    key_sum, value_sum, query_sum, output_sum, expand_sum, reduce_sum = done[2:8]
+    small_sums, expand_part = done[8:16], done[16]
     return (
         output[None],
         gradient[None],

time: 185 us -> 177 us (0.957)
  other arithmetic: 7.55 us -> 1.34 us
  local copies, waits for them, and re-layouts: 5.35 us -> 0.87 us
  Pallas kernels: 172 us -> 174 us
    convert_element_type x6 -> x0, other arithmetic: 6.2 us -> none  [fitted_shards(): t.astype(jnp.float32)]
    pallas_call x0 -> x1, Pallas kernels: none -> 4.87 us  [finish_call(): pl.pallas_call(finish_kernel, out_shape=passed + sums + [jax.ShapeDtypeSt...]
    pallas_call x1, Pallas kernels: 172 us -> 169 us  [layer_call(): pl.pallas_call(layer_kernel, out_shape=[jax.ShapeDtypeStruct((TOKENS, WID...]
where the time goes in v1:
time: 177 us
  Pallas kernels  174 us (98%)
    pallas_call x1, Pallas kernels, layer_call(): pl.pallas_call(layer_kernel, out_shape=[jax.ShapeDtypeStruct((TOKENS, WID...  169 us
    pallas_call x1, Pallas kernels, finish_call(): pl.pallas_call(finish_kernel, out_shape=passed + sums + [jax.ShapeDtypeSt...  4.87 us

profile of v1, /device:TPU:0, one launch (start us, length us, event | category | flops | bytes accessed | tf_op | source)
XLA Modules:
  0.0 177.1 jit_solution(1191245494692944670)
XLA Ops:
  0.7 0.1 pad.7.clone
  0.7 0.8 stack.35
  1.5 1.3 fusion.2.refs_6_
  2.9 169.2 %layer.1 = (bf16[256,768]{1,0:T(8,128)(2,1)}, f32[256,768]{1,0:T(8,128)}, bf16[96,768]{1,0:T(8,128)(2,1)}, bf16[96,768]{1,0:T(8,128)(2,1)}, bf16[96,768]{1,0:T(8...) custom-call(bf16[96,768]{1,0:T(8,128)(2,1)} %refs_0_.1, ...), custom_call_target="tpu_custom_call" | custom-call | tf_op jit(solution)/shard_map/layer/pallas_call | solution.py:1485
  172.1 4.9 %finish.1 = (bf16[256,768]{1,0:T(8,128)(2,1)}, f32[256,768]{1,0:T(8,128)}, f32[96,768]{1,0:T(8,128)}, f32[96,768]{1,0:T(8,128)}, f32[96,768]{1,0:T(8,128)}, /*in...) custom-call(bf16[256,768]{1,0:T(8,128)(2,1)} %get-tuple-element.43.r, ...), custom_call_target="tpu_custom_call" | custom-call | tf_op jit(solution)/shard_map/finish/pallas_call | solution.py:1539
  (1 shorter events, 0.0 us)
